TPU v7x, 32 devices: a whole 2x2x4 slice. The times are simulated.
32 devices in a mesh: ind: 4 (over y, x), var: 8 (over z, core).
Axes of the slice: x: 2, y: 2, z: 4, core: 2. Of those that a mesh axis runs over, the one named last changes fastest.
Arguments:
- genotypes: bfloat16 [1024, 393216], P('var', 'ind'), may hold values from -6 to 6, as said below
- residual: float32 [393216], P('ind'), may hold values from -6 to 6
- ancestry: int32 [393216], P('ind'), may hold values from 0 to 4, never falling along the last dimension, each value on 1 to 196608 neighbouring positions
- effects: float32 [5, 1024], P(None, 'var'), may hold values from -4 to 4
- prior_precision: float32 [5, 5], replicated, may hold values from -12 to 12, as said below
- noise_var: float32 [5], replicated, may hold values from 0.5 to 2
- block_index: int32 [3, 256], P(None, 'var'), may hold values from 0 to 127, as said below
- gaussians: float32 [3, 5, 256], P(None, None, 'var'), may hold values from -5 to 5
Outputs:
- new_residual: float32 [393216], P(('ind', 'var'))
- new_effects: float32 [5, 1024], P(None, 'var')
Inputs may be any that keep to these rules, and one draw needn't show every extreme that they name: Scaled genotypes; variants and individuals have different scales. `prior_precision`: symmetric positive definite. `block_index`: in each step the 32 entries held by one index of var are distinct rows among that index's 128 variants; rows 0 and 127 appear in every draw.
All inputs are finite; a program needn't handle non-finite values.
Results may differ from a plain program's by a relative error of at most 0.0003.
Values sent between devices are 32-bit elements; how exact they have to be, the bound alone decides.
No kernel may reach another device: no remote copies, remote signals or barrier semaphores. Data moves between devices by JAX's collectives and lax.ppermute only.
A program may use at most 128 MiB of HBM per device.

v0:
```python
import functools

import jax
import jax.numpy as jnp
from jax import lax
from jax.experimental import pallas as pl
from jax.experimental.pallas import tpu as pltpu
from jax.sharding import PartitionSpec as P


LANES = 128
SUB = 8
BLOCK = 8

f32, bf16, i32 = jnp.float32, jnp.bfloat16, jnp.int32
in_vmem = pl.BlockSpec(memory_space=pltpu.VMEM)
in_hbm = pl.BlockSpec(memory_space=pltpu.HBM)


def tile_lanes(tile, count=1):
    return pl.ds(pl.multiple_of(tile * LANES, count * LANES), count * LANES)


def row_of(ref, tile, rows):
    return jnp.broadcast_to(ref[pl.ds(tile, 1), :], (rows, LANES))


def lanes_iota(rows):
    return lax.broadcasted_iota(i32, (rows, LANES), 1)


def read_limits(limits, ancestries):
    return [limits[k, 0] for k in range(ancestries + 1)]


def ancestry_at(starts, column):
    return sum([(start <= column).astype(i32) for start in starts[1:-1]])


def pack_columns(columns):
    groups = columns[0].shape[0] // SUB
    stride = LANES // groups
    lane = lanes_iota(SUB)
    packed = jnp.zeros((SUB, LANES), f32)
    for k, column in enumerate(columns):
        for b in range(groups):
            packed = jnp.where(lane == stride * b + k, column[SUB * b : SUB * (b + 1)], packed)
    return packed


def pack_sums(sums):
    return pack_columns([jnp.sum(sums[k], axis=1, keepdims=True) for k in range(sums.shape[0])])


def unpack_column(packed, k, rows):
    stride = LANES // (rows // SUB)
    parts = [
        jnp.broadcast_to(packed[:, stride * b + k : stride * b + k + 1], (SUB, LANES))
        for b in range(rows // SUB)
    ]
    return jnp.concatenate(parts, axis=0)


def load_kernel(
    genotypes_hbm, residual_hbm, ancestry_hbm, index_hbm, prior_hbm, noise_var_hbm,
    rows_out, payload, limits, selected, consts, own,
    genotypes, residual, ancestry, index, prior, noise_var, squares, products, semaphores, small,
):
    ancestries, block, _ = products.shape
    total = rows_out.shape[0]
    steps = total // block
    tiles = residual.shape[0]
    chunks = semaphores.shape[0]
    per_chunk = tiles // chunks

    sources = (index_hbm, prior_hbm, noise_var_hbm, ancestry_hbm, residual_hbm)
    targets = (index, prior, noise_var, ancestry, residual)
    copies = [pltpu.make_async_copy(a, b, small.at[i]) for i, (a, b) in enumerate(zip(sources, targets))]
    for one in copies:
        one.start()

    def copy(i):
        part = tile_lanes(i * per_chunk, per_chunk)
        return pltpu.make_async_copy(genotypes_hbm.at[:, part], genotypes.at[:, part], semaphores.at[i])

    def start(i, carry):
        copy(i).start()
        return carry

    lax.fori_loop(0, chunks, start, 0)
    squares[...] = jnp.zeros_like(squares)
    products[...] = jnp.zeros_like(products)

    copies[0].wait()
    lane = lanes_iota(1)
    for s in range(steps):
        for c in range(block):
            selected[pl.ds(s * block + c, 1), :] = (lane == index[s, c]).astype(f32)
    copies[1].wait()
    copies[2].wait()
    for a in range(ancestries):
        for b in range(ancestries):
            consts[pl.ds(a * ancestries + b, 1), :] = jnp.full((1, LANES), prior[a, b], f32)
        row = ancestries * ancestries + a
        consts[pl.ds(row, 1), :] = 1.0 / jnp.full((1, LANES), noise_var[0, a], f32)

    copies[3].wait()
    starts = [0]
    for k in range(1, ancestries):
        starts.append(jnp.sum((ancestry[...] < k).astype(i32)))
    starts.append(tiles * LANES)
    for k, first in enumerate(starts):
        limits[pl.ds(k, 1), :] = jnp.full((1, LANES), first, i32)
    copies[4].wait()
    mine = pl.multiple_of(lax.axis_index("var") * own.shape[0], SUB)
    own[...] = residual[pl.ds(mine, own.shape[0]), :]
    choose = selected[...].astype(bf16)

    def gather(tile):
        picked = jnp.dot(choose, genotypes[:, tile_lanes(tile, BLOCK)], preferred_element_type=f32)
        rows_out[:, tile_lanes(tile, BLOCK)] = picked.astype(bf16)
        return picked

    def chunk_step(i, carry):
        copy(i).wait()
        base = i * per_chunk
        low = ancestry_at(starts, base * LANES)
        high = ancestry_at(starts, (base + per_chunk) * LANES - 1)

        @pl.when(low == high)
        def _():
            square = jnp.zeros((block, LANES), f32)
            product = jnp.zeros((block, LANES), f32)
            for g in range(per_chunk // BLOCK):
                tile = base + g * BLOCK
                picked = gather(tile)
                for t in range(BLOCK):
                    x = picked[:block, t * LANES : (t + 1) * LANES]
                    square = square + x * x
                    product = product + x * row_of(residual, tile + t, block)
            squares[low] += square
            products[low] += product

        @pl.when(low != high)
        def _():
            for g in range(per_chunk // BLOCK):
                gather(base + g * BLOCK)

            def mixed(g, carry):
                tile = base + g * BLOCK

                def one(k, carry):
                    square = jnp.zeros((block, LANES), f32)
                    product = jnp.zeros((block, LANES), f32)
                    for t in range(BLOCK):
                        mine = row_of(ancestry, tile + t, block) == k
                        x = rows_out[pl.ds(0, block), tile_lanes(tile + t)].astype(f32)
                        x = jnp.where(mine, x, 0.0)
                        square = square + x * x
                        product = product + x * row_of(residual, tile + t, block)
                    squares[k] += square
                    products[k] += product
                    return carry

                first = ancestry_at(starts, tile * LANES)
                last = ancestry_at(starts, (tile + BLOCK) * LANES - 1)
                lax.fori_loop(first, last + 1, one, 0)
                return carry

            lax.fori_loop(0, per_chunk // BLOCK, mixed, 0)

        return carry

    lax.fori_loop(0, chunks, chunk_step, 0)
    payload[pl.ds(0, SUB), :] = pack_sums(products)
    payload[pl.ds(SUB, SUB), :] = pack_sums(squares)


def tree_sum(values):
    while len(values) > 1:
        values = [values[i] + values[i + 1] for i in range(0, len(values), 2)]
    return values[0]


def factor_columns(packed, before, consts, rows, store):
    ancestries = len(before)
    norms = [unpack_column(packed, k, rows) for k in range(ancestries)]
    const = lambda i: jnp.broadcast_to(consts[pl.ds(i, 1), :], (rows, LANES))
    lower = {}
    for b in range(ancestries):
        for a in range(b, ancestries):
            total = const(a * ancestries + b)
            if a == b:
                total = total + norms[a] * const(ancestries * ancestries + a)
            for m in range(b):
                total = total - lower[a, m] * lower[b, m]
            lower[a, b] = 1.0 / jnp.sqrt(total) if a == b else total * lower[b, b]
            store[a * ancestries + b] = lower[a, b]
    for k in range(ancestries):
        store[ancestries * ancestries + k] = norms[k] * before[k]


def commit(effects, selected, fresh, out):
    hit = selected > 0.5
    taken = jnp.sum(selected, axis=0, keepdims=True) > 0.5
    for k in range(out.shape[0]):
        value = jnp.sum(jnp.where(hit, fresh[k], 0.0), axis=0, keepdims=True)
        out[pl.ds(k, 1), :] = jnp.where(taken, value, effects[pl.ds(k, 1), :])


def prepare_kernel(step, *refs):
    selected, effects, gaussians = refs[:3]
    ancestries = effects.shape[0]
    rows = gaussians.shape[2]
    mine = lambda s: selected[pl.ds(s * rows, rows), :]
    if step == 0:
        columns = refs[3]
    else:
        fresh, columns, new_effects = refs[3:]
        commit(effects, mine(step - 1), fresh, new_effects)
        effects = new_effects
    hit = mine(step) > 0.5
    side = lax.broadcasted_iota(i32, (rows, rows), 0) == lax.broadcasted_iota(i32, (rows, rows), 1)
    for k in range(ancestries):
        noise = jnp.broadcast_to(gaussians[k, pl.ds(step, 1), :], (rows, rows))
        noise = jnp.sum(jnp.where(side, noise, 0.0), axis=1, keepdims=True)
        columns[k] = jnp.broadcast_to(noise, (rows, LANES))
        old = jnp.where(hit, row_of(effects, k, rows), 0.0)
        columns[ancestries + k] = jnp.broadcast_to(jnp.sum(old, axis=1, keepdims=True), (rows, LANES))


def commit_kernel(step, selected, effects, fresh, out):
    rows = fresh.shape[1]
    commit(effects, selected[pl.ds(step * rows, rows), :], fresh, out)


def sublane_sums(tiles):
    row = lax.broadcasted_iota(i32, (SUB, LANES), 0)
    for half in (1, 2, 4):
        low = (row & half) == 0
        tiles = [
            jnp.where(low, a, b) + pltpu.roll(jnp.where(low, b, a), half, 0)
            for a, b in zip(tiles[::2], tiles[1::2])
        ]
    return tiles[0]


def block_spread(rows_ref, step, change, tile):
    rows = change[0].shape[0] * len(change)
    tiles = []
    for t in range(BLOCK):
        x = rows_ref[pl.ds(step * rows, rows), tile_lanes(tile + t)].astype(f32)
        products = [x[SUB * b : SUB * (b + 1)] * c for b, c in enumerate(change)]
        tiles.append(tree_sum(products))
    return sublane_sums(tiles)


def group_size(tiles):
    size = 32
    while tiles % size:
        size //= 2
    return size


def spread_half(step, odd, rows_ref, limits, change_ref, out):
    ancestries, rows, _ = change_ref.shape
    starts = read_limits(limits, ancestries)
    me = lax.axis_index("var")
    pairs, per_part = out.shape[0], out.shape[1]
    group = group_size(per_part)
    change_of = lambda k: [change_ref[k, pl.ds(SUB * b, SUB), :] for b in range(rows // SUB)]

    def spread(i, carry):
        pair, local = i // (per_part // group), (i % (per_part // group)) * group
        base = (me ^ (2 * pair + odd)) * per_part + local
        first = ancestry_at(starts, base * LANES)
        last = ancestry_at(starts, (base + group) * LANES - 1)
        place = lambda g: pl.ds(pl.multiple_of(local + g * BLOCK, BLOCK), BLOCK)

        @pl.when(first == last)
        def _():
            change = change_of(first)
            for g in range(group // BLOCK):
                out[pair, place(g), :] = block_spread(rows_ref, step, change, base + g * BLOCK)

        @pl.when(first != last)
        def _():
            def mixed(g, carry):
                tile = base + g * BLOCK
                column = (tile + lax.broadcasted_iota(i32, (BLOCK, LANES), 0)) * LANES + lanes_iota(BLOCK)

                def one(k, value):
                    mine = block_spread(rows_ref, step, change_of(k), tile)
                    return jnp.where(column >= limits[k, 0], mine, value)

                begin = ancestry_at(starts, tile * LANES)
                end = ancestry_at(starts, (tile + BLOCK) * LANES - 1)
                out[pair, place(g), :] = lax.fori_loop(begin, end + 1, one, jnp.zeros((BLOCK, LANES), f32))
                return carry

            lax.fori_loop(0, group // BLOCK, mixed, 0)

        return carry

    lax.fori_loop(0, pairs * (per_part // group), spread, 0)


def draw_kernel(step, payloads, rows_ref, limits, columns, consts, *refs):
    parts = refs[:payloads]
    send, fresh_out, change_ref, factor = refs[payloads:]
    ancestries, rows, _ = fresh_out.shape
    total = tree_sum([part[...] for part in parts])
    noise = [columns[k] for k in range(ancestries)]
    before = [columns[ancestries + k] for k in range(ancestries)]
    factor_columns(total[SUB:], before, consts, rows, factor)
    low = lambda a, b: factor[a * ancestries + b]
    forward = []
    for a in range(ancestries):
        value = unpack_column(total[:SUB], a, rows) + factor[ancestries * ancestries + a]
        value = value * row_of(consts, ancestries * ancestries + a, rows)
        for m in range(a):
            value = value - low(a, m) * forward[m]
        forward.append(value * low(a, a) + noise[a])
    fresh = [None] * ancestries
    for a in reversed(range(ancestries)):
        value = forward[a]
        for m in range(a + 1, ancestries):
            value = value - low(m, a) * fresh[m]
        fresh[a] = value * low(a, a)
        fresh_out[a] = fresh[a]
        change_ref[a] = fresh[a] - before[a]
    spread_half(step, 1, rows_ref, limits, change_ref, send)


def keep_kernel(step, rows_ref, limits, change_ref, out):
    spread_half(step, 0, rows_ref, limits, change_ref, out)


def pair_kernel(keep, received, *outs):
    for pair, out in enumerate(outs):
        out[...] = keep[pair] + received[pair]


def chip_kernel(count, old, *refs):
    parts, out = refs[:count], refs[-1]
    out[...] = old[...] - tree_sum([part[...] for part in parts])


def segment_sums(step, rows_ref, limits, sums, tiles, base_of, residual=None):
    ancestries, rows, _ = sums.shape
    starts = read_limits(limits, ancestries)
    group = group_size(tiles)

    def body(i, carry):
        base = base_of(i * group)
        first = ancestry_at(starts, base * LANES)
        last = ancestry_at(starts, (base + group) * LANES - 1)

        def one(t, k=None):
            x = rows_ref[pl.ds(step * rows, rows), tile_lanes(base + t)].astype(f32)
            other = x if residual is None else row_of(residual, i * group + t, rows)
            if k is not None:
                column = (base + t) * LANES + lanes_iota(1)
                mine = (column >= limits[k, 0]) & (column < limits[k + 1, 0])
                x = jnp.where(jnp.broadcast_to(mine, x.shape), x, 0.0)
            return x * other

        @pl.when(first == last)
        def _():
            total = jnp.zeros((rows, LANES), f32)
            for t in range(group):
                total = total + one(t)
            sums[first] += total

        @pl.when(first != last)
        def _():
            def mixed(g, carry):
                def each(k, carry):
                    total = jnp.zeros((rows, LANES), f32)
                    for t in range(BLOCK):
                        total = total + one(g * BLOCK + t, k)
                    sums[k] += total
                    return carry

                begin = ancestry_at(starts, (base + g * BLOCK) * LANES)
                end = ancestry_at(starts, (base + (g + 1) * BLOCK) * LANES - 1)
                lax.fori_loop(begin, end + 1, each, 0)
                return carry

            lax.fori_loop(0, group // BLOCK, mixed, 0)

        return carry

    lax.fori_loop(0, residual.shape[0] // group if residual is not None else tiles // group, body, 0)


def norms_kernel(step, rows_ref, limits, out, sums):
    sums[...] = jnp.zeros_like(sums)
    tiles = rows_ref.shape[1] // LANES
    segment_sums(step, rows_ref, limits, sums, tiles, lambda local: local)
    out[...] = pack_sums(sums)


def scores_kernel(step, count, scale, shift, first, last, rows_ref, limits, *refs):
    parts, rest = refs[:count], refs[count:]
    residual = rest[-1] if not last else rest[-2]
    sums = rest[-2] if not last else rest[-1]
    sums[...] = jnp.zeros_like(sums) if first else rest[0][...]
    per_part = parts[0].shape[0]
    for p, part in enumerate(parts):
        residual[pl.ds(p * per_part, per_part), :] = part[...]
    me = lax.axis_index("var")
    base_of = lambda local: (me ^ (scale * (local // per_part) + shift)) * per_part + local % per_part
    segment_sums(step, rows_ref, limits, sums, per_part, base_of, residual)
    if last:
        norms, out = rest[1:3]
        out[pl.ds(0, SUB), :] = pack_sums(sums)
        out[pl.ds(SUB, SUB), :] = norms[...]


def call(kernel, outs, inputs, scratch=(), limit=8, specs=None):
    return pl.pallas_call(
        kernel,
        out_shape=outs,
        in_specs=specs or [in_vmem] * len(inputs),
        out_specs=jax.tree.map(lambda out: in_vmem, outs),
        scratch_shapes=list(scratch),
        compiler_params=pltpu.CompilerParams(vmem_limit_bytes=limit << 20),
    )(*inputs)


def exchange(array, axis, offset):
    size = lax.axis_size(axis)
    return lax.ppermute(array, axis, [(i, i ^ offset) for i in range(size)])


def gather_ind(array):
    parts, offset = [array], 1
    while offset < lax.axis_size("ind"):
        parts = parts + [exchange(part, "ind", offset) for part in parts]
        offset *= 2
    return parts


def update(
    genotypes, residual, ancestry, effects, prior_precision, noise_var, block_index, gaussians
):
    ancestries, variants = effects.shape
    steps, block = block_index.shape
    people = residual.shape[0]
    var_size = lax.axis_size("var")
    chips = var_size // 2
    tiles = people // LANES
    part = tiles // var_size
    per_chunk = 64
    while tiles % per_chunk:
        per_chunk //= 2
    shape = jax.ShapeDtypeStruct
    in_place = lambda array: pltpu.with_memory_space_constraint(array, pltpu.HBM)
    residual = residual.reshape(tiles, LANES)
    ancestry = ancestry.reshape(tiles, LANES)
    noise_var = noise_var.reshape(1, ancestries)
    gaussians = gaussians.transpose(1, 0, 2)
    inputs = [genotypes, residual, ancestry, block_index, prior_precision, noise_var]

    held, payload, limits, selected, consts, current = call(
        load_kernel,
        (
            pltpu.VMEM((steps * block, people), bf16),
            shape((2 * SUB, LANES), f32),
            shape((SUB, LANES), i32),
            shape((steps * block, variants), f32),
            shape((ancestries * (ancestries + 1), LANES), f32),
            shape((part, LANES), f32),
        ),
        [in_place(array) for array in inputs],
        [
            pltpu.VMEM(genotypes.shape, bf16),
            pltpu.VMEM(residual.shape, f32),
            pltpu.VMEM(ancestry.shape, i32),
            pltpu.SMEM(block_index.shape, i32),
            pltpu.SMEM(prior_precision.shape, f32),
            pltpu.SMEM(noise_var.shape, f32),
            pltpu.VMEM((ancestries, block, LANES), f32),
            pltpu.VMEM((ancestries, block, LANES), f32),
            pltpu.SemaphoreType.DMA((tiles // per_chunk,)),
            pltpu.SemaphoreType.DMA((5,)),
        ],
        32,
        [in_hbm] * len(inputs),
    )
    held = pltpu.with_memory_space_constraint(held, pltpu.VMEM)

    columns_shape = shape((2 * ancestries, block, LANES), f32)
    column_shape = shape((ancestries, block, LANES), f32)
    part_shape = shape((chips, part, LANES), f32)
    effects_shape = shape(effects.shape, f32)
    factor = pltpu.VMEM((ancestries * (ancestries + 1), block, LANES), f32)
    sums_scratch = pltpu.VMEM(column_shape.shape, f32)
    residual_scratch = pltpu.VMEM(((chips - 1) * part, LANES), f32)
    fresh = None
    for s in range(steps):
        if s == 0:
            columns = call(functools.partial(prepare_kernel, s), columns_shape, [selected, effects, gaussians])
        else:
            columns, effects = call(
                functools.partial(prepare_kernel, s),
                (columns_shape, effects_shape),
                [selected, effects, gaussians, fresh],
            )
        parts = gather_ind(payload)
        send, fresh, change = call(
            functools.partial(draw_kernel, s, len(parts)),
            (part_shape, column_shape, column_shape),
            [held, limits, columns, consts, *parts],
            [factor],
        )
        received = exchange(send, "var", 1)
        keep = call(functools.partial(keep_kernel, s), part_shape, [held, limits, change])
        sums = call(pair_kernel, (shape((part, LANES), f32),) * chips, [keep, received])
        arrived = [sums[0]] + [exchange(sums[e], "var", 2 * e) for e in range(1, chips)]
        norms = []
        if s + 1 < steps:
            kernel = functools.partial(norms_kernel, s + 1)
            norms = [call(kernel, shape((SUB, LANES), f32), [held, limits], [sums_scratch])]
        kernel = functools.partial(chip_kernel, chips)
        current = call(kernel, shape((part, LANES), f32), [current, *arrived, *norms])
        if s + 1 == steps:
            effects = call(functools.partial(commit_kernel, s), effects_shape, [selected, effects, fresh])
            break
        even = [current] + [exchange(current, "var", 2 * e) for e in range(1, chips)]
        odd = [exchange(one, "var", 1) for one in even]
        scores = functools.partial(scores_kernel, s + 1)
        partial = call(
            functools.partial(scores, 2, 1, 0, True, False),
            column_shape,
            [held, limits, even[0], odd[0]],
            [pltpu.VMEM((2 * part, LANES), f32)],
        )
        partial = call(
            functools.partial(scores, chips - 1, 2, 2, False, False),
            column_shape,
            [held, limits, *even[1:], partial],
            [residual_scratch],
        )
        payload = call(
            functools.partial(scores, chips - 1, 2, 3, False, True),
            shape((2 * SUB, LANES), f32),
            [held, limits, *odd[1:], partial, *norms],
            [residual_scratch, sums_scratch],
        )
    return current.reshape(-1), effects


def solution(mesh):
    return jax.shard_map(
        update,
        mesh=mesh,
        in_specs=(
            P("var", "ind"),
            P("ind"),
            P("ind"),
            P(None, "var"),
            P(),
            P(),
            P(None, "var"),
            P(None, None, "var"),
        ),
        out_specs=(P(("ind", "var")), P(None, "var")),
        check_vma=False,
    )
```

profile of v0, /device:TPU:0, one launch (start us, length us, event | category | flops | bytes accessed | tf_op | source)
XLA Modules:
  0.0 96.2 jit_solution(16770006581916548632)
XLA Ops:
  0.7 10.2 %shard_map.95 = (bf16[96,98304]{1,0:T(8,128)(2,1)S(1)}, f32[16,128]{1,0:T(8,128)S(1)}, s32[8,128]{1,0:T(8,128)S(1)}, f32[96,128]{1,0:T(8,128)S(1)}, f32[30,128]{1,0:T(8,128)S(1)}, /*index=5*/f32[96,128]{1,0:T(8,128)S(1)}) custom-call(bf16[128,98304]{1,0:T(8,128)(2,1)} %genotypes_hbm.1, f32[768,128]{1,0:T(8,128)} %bitcast.8, s32[768,128]{1,0:T(8,128)} %bitcast.9, ...), custom_call_target="tpu_custom_call" | custom-call | tf_op jit(solution)/shard_map/pallas_call | solution.py:422
  10.8 2.7 %collective-permute-start = (f32[16,128]{1,0:T(8,128)S(1)}, f32[16,128]{1,0:T(8,128)S(1)}, u32[]{:S(2)}, u32[]{:S(2)}) collective-permute-start(f32[16,128]{1,0:T(8,128)S(1)} %get-tuple-element.38.refs_0_), channel_id=1, source_target_pairs={{0,8},{8,0},{16,24},{24,16},{1,9},{9,1},{17,25},{25,17},{2,10},{10... | collective-permute-start | bytes 24584 | tf_op jit(solution)/shard_map/ppermute | solution.py:434
  15.1 1.6 %collective-permute-start.2 = (f32[16,128]{1,0:T(8,128)S(1)}, f32[16,128]{1,0:T(8,128)S(1)}, u32[]{:S(2)}, u32[]{:S(2)}) collective-permute-start(f32[16,128]{1,0:T(8,128)S(1)} %collective-permute-done.refs_1_), channel_id=1, source_target_pairs={{0,16},{8,24},{16,0},{24,8},{1,17},{9,25},{17,1},{25,9},{2,18},{10... | collective-permute-start | bytes 24584 | tf_op jit(solution)/shard_map/ppermute | solution.py:434
  17.1 1.6 %collective-permute-done.2.refs_3_ = f32[16,128]{1,0:T(8,128)S(1)} collective-permute-done((f32[16,128]{1,0:T(8,128)S(1)}, f32[16,128]{1,0:T(8,128)S(1)}, u32[]{:S(2)}, u32[]{:S(2)}) %collective-permute-start.2) | collective-permute-done | bytes 8224 | tf_op jit(solution)/shard_map/ppermute | solution.py:434
  18.8 1.6 %shard_map.97 = (f32[4,96,128]{2,1,0:T(8,128)S(1)}, f32[5,32,128]{2,1,0:T(8,128)S(1)}, f32[5,32,128]{2,1,0:T(8,128)S(1)}) custom-call(bf16[96,98304]{1,0:T(8,128)(2,1)S(1)} %get-tuple-element.34.rows_ref, s32[8,128]{1,0:T(8,128)S(1)} %get-tuple-element.35.limits, f32[10,32,128]{2,1,0:T(8,128)S(1)} %shard_map.96.columns, ...), custom_call_target="tpu_custom_call" | custom-call | tf_op jit(solution)/shard_map/pallas_call | solution.py:422
  20.4 1.8 %shard_map.98.keep = f32[4,96,128]{2,1,0:T(8,128)S(1)} custom-call(bf16[96,98304]{1,0:T(8,128)(2,1)S(1)} %get-tuple-element.34.rows_ref, s32[8,128]{1,0:T(8,128)S(1)} %get-tuple-element.35.limits, f32[5,32,128]{2,1,0:T(8,128)S(1)} %get-tuple-element.39.change_ref), custom_call_target="tpu_custom_call" | custom-call | tf_op jit(solution)/shard_map/pallas_call | solution.py:422
  22.3 2.5 %collective-permute-start.4 = (f32[96,128]{1,0:T(8,128)S(1)}, f32[96,128]{1,0:T(8,128)S(1)}, u32[]{:S(2)}, u32[]{:S(2)}) collective-permute-start(f32[96,128]{1,0:T(8,128)S(1)} %get-tuple-element.42), channel_id=1, source_target_pairs={{0,2},{1,3},{2,0},{3,1},{4,6},{5,7},{6,4},{7,5},{8,10},{9,11},{10,... | collective-permute-start | bytes 147464 | tf_op jit(solution)/shard_map/ppermute | solution.py:434
  24.8 2.6 %collective-permute-start.5 = (f32[96,128]{1,0:T(8,128)S(1)}, f32[96,128]{1,0:T(8,128)S(1)}, u32[]{:S(2)}, u32[]{:S(2)}) collective-permute-start(f32[96,128]{1,0:T(8,128)S(1)} %get-tuple-element.43), channel_id=1, source_target_pairs={{0,4},{1,5},{2,6},{3,7},{4,0},{5,1},{6,2},{7,3},{8,12},{9,13},{10,... | collective-permute-start | bytes 147464 | tf_op jit(solution)/shard_map/ppermute | solution.py:434
  27.4 3.4 %shard_map.100.refs_4_ = f32[8,128]{1,0:T(8,128)S(1)} custom-call(bf16[96,98304]{1,0:T(8,128)(2,1)S(1)} %get-tuple-element.34.rows_ref, s32[8,128]{1,0:T(8,128)S(1)} %get-tuple-element.35.limits), custom_call_target="tpu_custom_call" | custom-call | tf_op jit(solution)/shard_map/pallas_call | solution.py:422
  30.8 2.5 %collective-permute-done.6.refs_3_ = f32[96,128]{1,0:T(8,128)S(1)} collective-permute-done((f32[96,128]{1,0:T(8,128)S(1)}, f32[96,128]{1,0:T(8,128)S(1)}, u32[]{:S(2)}, u32[]{:S(2)}) %collective-permute-start.6) | collective-permute-done | bytes 49184 | tf_op jit(solution)/shard_map/ppermute | solution.py:434
  34.8 2.0 %collective-permute-start.7 = (f32[96,128]{1,0:T(8,128)S(1)}, f32[96,128]{1,0:T(8,128)S(1)}, u32[]{:S(2)}, u32[]{:S(2)}) collective-permute-start(f32[96,128]{1,0:T(8,128)S(1)} %shard_map.101.refs_0_.old), channel_id=1, source_target_pairs={{0,2},{1,3},{2,0},{3,1},{4,6},{5,7},{6,4},{7,5},{8,10},{9,11},{10,... | collective-permute-start | bytes 147464 | tf_op jit(solution)/shard_map/ppermute | solution.py:434
  36.9 1.5 %collective-permute-done.9.refs_1_ = f32[96,128]{1,0:T(8,128)S(1)} collective-permute-done((f32[96,128]{1,0:T(8,128)S(1)}, f32[96,128]{1,0:T(8,128)S(1)}, u32[]{:S(2)}, u32[]{:S(2)}) %collective-permute-start.9) | collective-permute-done | bytes 49184 | tf_op jit(solution)/shard_map/ppermute | solution.py:434
  41.6 1.6 %shard_map.104.refs_3_ = f32[5,32,128]{2,1,0:T(8,128)S(1)} custom-call(bf16[96,98304]{1,0:T(8,128)(2,1)S(1)} %get-tuple-element.34.rows_ref, s32[8,128]{1,0:T(8,128)S(1)} %get-tuple-element.35.limits, f32[96,128]{1,0:T(8,128)S(1)} %collective-permute-done.7.refs_0_, f32[96,128]{1,0:T(8,128)S(1)} %collective-permute-done.9.refs_1_, ...), custom_call_target="tpu_custom_call" | custom-call | tf_op jit(solution)/shard_map/pallas_call | solution.py:422
  46.3 2.0 %collective-permute-done.14.refs_1_ = f32[16,128]{1,0:T(8,128)S(1)} collective-permute-done((f32[16,128]{1,0:T(8,128)S(1)}, f32[16,128]{1,0:T(8,128)S(1)}, u32[]{:S(2)}, u32[]{:S(2)}) %collective-permute-start.14) | collective-permute-done | bytes 8224 | tf_op jit(solution)/shard_map/ppermute | solution.py:434
  49.6 2.4 %collective-permute-done.16.refs_3_ = f32[16,128]{1,0:T(8,128)S(1)} collective-permute-done((f32[16,128]{1,0:T(8,128)S(1)}, f32[16,128]{1,0:T(8,128)S(1)}, u32[]{:S(2)}, u32[]{:S(2)}) %collective-permute-start.16) | collective-permute-done | bytes 8224 | tf_op jit(solution)/shard_map/ppermute | solution.py:434
  52.0 1.6 %shard_map.106 = (f32[4,96,128]{2,1,0:T(8,128)S(1)}, f32[5,32,128]{2,1,0:T(8,128)S(1)}, f32[5,32,128]{2,1,0:T(8,128)S(1)}) custom-call(bf16[96,98304]{1,0:T(8,128)(2,1)S(1)} %get-tuple-element.34.rows_ref, s32[8,128]{1,0:T(8,128)S(1)} %get-tuple-element.35.limits, f32[10,32,128]{2,1,0:T(8,128)S(1)} %get-tuple-element.46.columns, ...), custom_call_target="tpu_custom_call" | custom-call | tf_op jit(solution)/shard_map/pallas_call | solution.py:422
  53.7 1.8 %shard_map.107.keep = f32[4,96,128]{2,1,0:T(8,128)S(1)} custom-call(bf16[96,98304]{1,0:T(8,128)(2,1)S(1)} %get-tuple-element.34.rows_ref, s32[8,128]{1,0:T(8,128)S(1)} %get-tuple-element.35.limits, f32[5,32,128]{2,1,0:T(8,128)S(1)} %get-tuple-element.47.change_ref), custom_call_target="tpu_custom_call" | custom-call | tf_op jit(solution)/shard_map/pallas_call | solution.py:422
  56.2 1.5 %collective-permute-start.19 = (f32[96,128]{1,0:T(8,128)S(1)}, f32[96,128]{1,0:T(8,128)S(1)}, u32[]{:S(2)}, u32[]{:S(2)}) collective-permute-start(f32[96,128]{1,0:T(8,128)S(1)} %get-tuple-element.51), channel_id=1, source_target_pairs={{0,4},{1,5},{2,6},{3,7},{4,0},{5,1},{6,2},{7,3},{8,12},{9,13},{10,... | collective-permute-start | bytes 147464 | tf_op jit(solution)/shard_map/ppermute | solution.py:434
  57.7 2.3 %collective-permute-start.20 = (f32[96,128]{1,0:T(8,128)S(1)}, f32[96,128]{1,0:T(8,128)S(1)}, u32[]{:S(2)}, u32[]{:S(2)}) collective-permute-start(f32[96,128]{1,0:T(8,128)S(1)} %get-tuple-element.52), channel_id=1, source_target_pairs={{0,6},{1,7},{2,4},{3,5},{4,2},{5,3},{6,0},{7,1},{8,14},{9,15},{10,... | collective-permute-start | bytes 147464 | tf_op jit(solution)/shard_map/ppermute | solution.py:434
  60.0 3.4 %shard_map.109.refs_4_ = f32[8,128]{1,0:T(8,128)S(1)} custom-call(bf16[96,98304]{1,0:T(8,128)(2,1)S(1)} %get-tuple-element.34.rows_ref, s32[8,128]{1,0:T(8,128)S(1)} %get-tuple-element.35.limits), custom_call_target="tpu_custom_call" | custom-call | tf_op jit(solution)/shard_map/pallas_call | solution.py:422
  64.3 2.2 %collective-permute-start.23 = (f32[96,128]{1,0:T(8,128)S(1)}, f32[96,128]{1,0:T(8,128)S(1)}, u32[]{:S(2)}, u32[]{:S(2)}) collective-permute-start(f32[96,128]{1,0:T(8,128)S(1)} %shard_map.110.refs_0_.old), channel_id=1, source_target_pairs={{0,4},{1,5},{2,6},{3,7},{4,0},{5,1},{6,2},{7,3},{8,12},{9,13},{10,... | collective-permute-start | bytes 147464 | tf_op jit(solution)/shard_map/ppermute | solution.py:434
  66.5 1.5 %collective-permute-start.25 = (f32[96,128]{1,0:T(8,128)S(1)}, f32[96,128]{1,0:T(8,128)S(1)}, u32[]{:S(2)}, u32[]{:S(2)}) collective-permute-start(f32[96,128]{1,0:T(8,128)S(1)} %shard_map.110.refs_0_.old), channel_id=1, source_target_pairs={{0,6},{1,7},{2,4},{3,5},{4,2},{5,3},{6,0},{7,1},{8,14},{9,15},{10,... | collective-permute-start | bytes 147464 | tf_op jit(solution)/shard_map/ppermute | solution.py:434
  68.6 1.8 %collective-permute-done.23.refs_1_ = f32[96,128]{1,0:T(8,128)S(1)} collective-permute-done((f32[96,128]{1,0:T(8,128)S(1)}, f32[96,128]{1,0:T(8,128)S(1)}, u32[]{:S(2)}, u32[]{:S(2)}) %collective-permute-start.23) | collective-permute-done | bytes 49184 | tf_op jit(solution)/shard_map/ppermute | solution.py:434
  70.3 2.1 %collective-permute-done.25.refs_2_ = f32[96,128]{1,0:T(8,128)S(1)} collective-permute-done((f32[96,128]{1,0:T(8,128)S(1)}, f32[96,128]{1,0:T(8,128)S(1)}, u32[]{:S(2)}, u32[]{:S(2)}) %collective-permute-start.25) | collective-permute-done | bytes 49184 | tf_op jit(solution)/shard_map/ppermute | solution.py:434
  73.6 1.6 %shard_map.113.refs_3_ = f32[5,32,128]{2,1,0:T(8,128)S(1)} custom-call(bf16[96,98304]{1,0:T(8,128)(2,1)S(1)} %get-tuple-element.34.rows_ref, s32[8,128]{1,0:T(8,128)S(1)} %get-tuple-element.35.limits, f32[96,128]{1,0:T(8,128)S(1)} %collective-permute-done.21.refs_0_, f32[96,128]{1,0:T(8,128)S(1)} %collective-permute-done.23.refs_1_, ...), custom_call_target="tpu_custom_call" | custom-call | tf_op jit(solution)/shard_map/pallas_call | solution.py:422
  77.5 2.9 %collective-permute-done.28.refs_1_ = f32[16,128]{1,0:T(8,128)S(1)} collective-permute-done((f32[16,128]{1,0:T(8,128)S(1)}, f32[16,128]{1,0:T(8,128)S(1)}, u32[]{:S(2)}, u32[]{:S(2)}) %collective-permute-start.28) | collective-permute-done | bytes 8224 | tf_op jit(solution)/shard_map/ppermute | solution.py:434
  81.1 2.9 %collective-permute-done.30.refs_3_ = f32[16,128]{1,0:T(8,128)S(1)} collective-permute-done((f32[16,128]{1,0:T(8,128)S(1)}, f32[16,128]{1,0:T(8,128)S(1)}, u32[]{:S(2)}, u32[]{:S(2)}) %collective-permute-start.30) | collective-permute-done | bytes 8224 | tf_op jit(solution)/shard_map/ppermute | solution.py:434
  84.0 1.6 %shard_map.115 = (f32[4,96,128]{2,1,0:T(8,128)S(1)}, f32[5,32,128]{2,1,0:T(8,128)S(1)}, f32[5,32,128]{2,1,0:T(8,128)S(1)}) custom-call(bf16[96,98304]{1,0:T(8,128)(2,1)S(1)} %get-tuple-element.34.rows_ref, s32[8,128]{1,0:T(8,128)S(1)} %get-tuple-element.35.limits, f32[10,32,128]{2,1,0:T(8,128)S(1)} %get-tuple-element.55.columns, ...), custom_call_target="tpu_custom_call" | custom-call | tf_op jit(solution)/shard_map/pallas_call | solution.py:422
  85.7 1.8 %shard_map.116.keep = f32[4,96,128]{2,1,0:T(8,128)S(1)} custom-call(bf16[96,98304]{1,0:T(8,128)(2,1)S(1)} %get-tuple-element.34.rows_ref, s32[8,128]{1,0:T(8,128)S(1)} %get-tuple-element.35.limits, f32[5,32,128]{2,1,0:T(8,128)S(1)} %get-tuple-element.56.change_ref), custom_call_target="tpu_custom_call" | custom-call | tf_op jit(solution)/shard_map/pallas_call | solution.py:422
  87.6 2.1 %collective-permute-start.33 = (f32[96,128]{1,0:T(8,128)S(1)}, f32[96,128]{1,0:T(8,128)S(1)}, u32[]{:S(2)}, u32[]{:S(2)}) collective-permute-start(f32[96,128]{1,0:T(8,128)S(1)} %get-tuple-element.60), channel_id=1, source_target_pairs={{0,4},{1,5},{2,6},{3,7},{4,0},{5,1},{6,2},{7,3},{8,12},{9,13},{10,... | collective-permute-start | bytes 147464 | tf_op jit(solution)/shard_map/ppermute | solution.py:434
  89.7 2.3 %collective-permute-start.34 = (f32[96,128]{1,0:T(8,128)S(1)}, f32[96,128]{1,0:T(8,128)S(1)}, u32[]{:S(2)}, u32[]{:S(2)}) collective-permute-start(f32[96,128]{1,0:T(8,128)S(1)} %get-tuple-element.61), channel_id=1, source_target_pairs={{0,6},{1,7},{2,4},{3,5},{4,2},{5,3},{6,0},{7,1},{8,14},{9,15},{10,... | collective-permute-start | bytes 147464 | tf_op jit(solution)/shard_map/ppermute | solution.py:434
  93.4 2.2 %collective-permute-done.34.refs_3_ = f32[96,128]{1,0:T(8,128)S(1)} collective-permute-done((f32[96,128]{1,0:T(8,128)S(1)}, f32[96,128]{1,0:T(8,128)S(1)}, u32[]{:S(2)}, u32[]{:S(2)}) %collective-permute-start.34) | collective-permute-done | bytes 49184 | tf_op jit(solution)/shard_map/ppermute | solution.py:434
  (67 shorter events, 19.7 us)
Async XLA Ops:
  10.8 4.3 %collective-permute-start = (f32[16,128]{1,0:T(8,128)S(1)}, f32[16,128]{1,0:T(8,128)S(1)}, u32[]{:S(2)}, u32[]{:S(2)}) collective-permute-start(f32[16,128]{1,0:T(8,128)S(1)} %get-tuple-element.38.refs_0_), channel_id=1, source_target_pairs={{0,8},{8,0},{16,24},{24,16},{1,9},{9,1},{17,25},{25,17},{2,10},{10... | collective-permute-start | bytes 24584 | tf_op jit(solution)/shard_map/ppermute | solution.py:434
  13.5 3.7 %collective-permute-start.1 = (f32[16,128]{1,0:T(8,128)S(1)}, f32[16,128]{1,0:T(8,128)S(1)}, u32[]{:S(2)}, u32[]{:S(2)}) collective-permute-start(f32[16,128]{1,0:T(8,128)S(1)} %get-tuple-element.38.refs_0_), channel_id=1, source_target_pairs={{0,16},{8,24},{16,0},{24,8},{1,17},{9,25},{17,1},{25,9},{2,18},{10... | collective-permute-start | bytes 24584 | tf_op jit(solution)/shard_map/ppermute | solution.py:434
  15.1 3.7 %collective-permute-start.2 = (f32[16,128]{1,0:T(8,128)S(1)}, f32[16,128]{1,0:T(8,128)S(1)}, u32[]{:S(2)}, u32[]{:S(2)}) collective-permute-start(f32[16,128]{1,0:T(8,128)S(1)} %collective-permute-done.refs_1_), channel_id=1, source_target_pairs={{0,16},{8,24},{16,0},{24,8},{1,17},{9,25},{17,1},{25,9},{2,18},{10... | collective-permute-start | bytes 24584 | tf_op jit(solution)/shard_map/ppermute | solution.py:434
  22.3 8.5 %collective-permute-start.4 = (f32[96,128]{1,0:T(8,128)S(1)}, f32[96,128]{1,0:T(8,128)S(1)}, u32[]{:S(2)}, u32[]{:S(2)}) collective-permute-start(f32[96,128]{1,0:T(8,128)S(1)} %get-tuple-element.42), channel_id=1, source_target_pairs={{0,2},{1,3},{2,0},{3,1},{4,6},{5,7},{6,4},{7,5},{8,10},{9,11},{10,... | collective-permute-start | bytes 147464 | tf_op jit(solution)/shard_map/ppermute | solution.py:434
  24.8 6.0 %collective-permute-start.5 = (f32[96,128]{1,0:T(8,128)S(1)}, f32[96,128]{1,0:T(8,128)S(1)}, u32[]{:S(2)}, u32[]{:S(2)}) collective-permute-start(f32[96,128]{1,0:T(8,128)S(1)} %get-tuple-element.43), channel_id=1, source_target_pairs={{0,4},{1,5},{2,6},{3,7},{4,0},{5,1},{6,2},{7,3},{8,12},{9,13},{10,... | collective-permute-start | bytes 147464 | tf_op jit(solution)/shard_map/ppermute | solution.py:434
  27.4 5.9 %collective-permute-start.6 = (f32[96,128]{1,0:T(8,128)S(1)}, f32[96,128]{1,0:T(8,128)S(1)}, u32[]{:S(2)}, u32[]{:S(2)}) collective-permute-start(f32[96,128]{1,0:T(8,128)S(1)} %get-tuple-element.44), channel_id=1, source_target_pairs={{0,6},{1,7},{2,4},{3,5},{4,2},{5,3},{6,0},{7,1},{8,14},{9,15},{10,... | collective-permute-start | bytes 147464 | tf_op jit(solution)/shard_map/ppermute | solution.py:434
  33.3 5.1 %collective-permute-start.9 = (f32[96,128]{1,0:T(8,128)S(1)}, f32[96,128]{1,0:T(8,128)S(1)}, u32[]{:S(2)}, u32[]{:S(2)}) collective-permute-start(f32[96,128]{1,0:T(8,128)S(1)} %shard_map.101.refs_0_.old), channel_id=1, source_target_pairs={{0,4},{1,5},{2,6},{3,7},{4,0},{5,1},{6,2},{7,3},{8,12},{9,13},{10,... | collective-permute-start | bytes 147464 | tf_op jit(solution)/shard_map/ppermute | solution.py:434
  34.0 5.9 %collective-permute-start.11 = (f32[96,128]{1,0:T(8,128)S(1)}, f32[96,128]{1,0:T(8,128)S(1)}, u32[]{:S(2)}, u32[]{:S(2)}) collective-permute-start(f32[96,128]{1,0:T(8,128)S(1)} %shard_map.101.refs_0_.old), channel_id=1, source_target_pairs={{0,6},{1,7},{2,4},{3,5},{4,2},{5,3},{6,0},{7,1},{8,14},{9,15},{10,... | collective-permute-start | bytes 147464 | tf_op jit(solution)/shard_map/ppermute | solution.py:434
  34.8 5.0 %collective-permute-start.7 = (f32[96,128]{1,0:T(8,128)S(1)}, f32[96,128]{1,0:T(8,128)S(1)}, u32[]{:S(2)}, u32[]{:S(2)}) collective-permute-start(f32[96,128]{1,0:T(8,128)S(1)} %shard_map.101.refs_0_.old), channel_id=1, source_target_pairs={{0,2},{1,3},{2,0},{3,1},{4,6},{5,7},{6,4},{7,5},{8,10},{9,11},{10,... | collective-permute-start | bytes 147464 | tf_op jit(solution)/shard_map/ppermute | solution.py:434
  36.9 3.5 %collective-permute-start.13 = (f32[96,128]{1,0:T(8,128)S(1)}, f32[96,128]{1,0:T(8,128)S(1)}, u32[]{:S(2)}, u32[]{:S(2)}) collective-permute-start(f32[96,128]{1,0:T(8,128)S(1)} %shard_map.101.refs_0_.old), channel_id=1, source_target_pairs={{0,1},{1,0},{2,3},{3,2},{4,5},{5,4},{6,7},{7,6},{8,9},{9,8},{10,11... | collective-permute-start | bytes 147464 | tf_op jit(solution)/shard_map/ppermute | solution.py:434
  38.4 4.8 %collective-permute-start.10 = (f32[96,128]{1,0:T(8,128)S(1)}, f32[96,128]{1,0:T(8,128)S(1)}, u32[]{:S(2)}, u32[]{:S(2)}) collective-permute-start(f32[96,128]{1,0:T(8,128)S(1)} %collective-permute-done.9.refs_1_), channel_id=1, source_target_pairs={{0,1},{1,0},{2,3},{3,2},{4,5},{5,4},{6,7},{7,6},{8,9},{9,8},{10,11... | collective-permute-start | bytes 147464 | tf_op jit(solution)/shard_map/ppermute | solution.py:434
  39.9 3.3 %collective-permute-start.12 = (f32[96,128]{1,0:T(8,128)S(1)}, f32[96,128]{1,0:T(8,128)S(1)}, u32[]{:S(2)}, u32[]{:S(2)}) collective-permute-start(f32[96,128]{1,0:T(8,128)S(1)} %collective-permute-done.11.refs_2_), channel_id=1, source_target_pairs={{0,1},{1,0},{2,3},{3,2},{4,5},{5,4},{6,7},{7,6},{8,9},{9,8},{10,11... | collective-permute-start | bytes 147464 | tf_op jit(solution)/shard_map/ppermute | solution.py:434
  39.9 3.3 %collective-permute-start.8 = (f32[96,128]{1,0:T(8,128)S(1)}, f32[96,128]{1,0:T(8,128)S(1)}, u32[]{:S(2)}, u32[]{:S(2)}) collective-permute-start(f32[96,128]{1,0:T(8,128)S(1)} %collective-permute-done.7.refs_0_), channel_id=1, source_target_pairs={{0,1},{1,0},{2,3},{3,2},{4,5},{5,4},{6,7},{7,6},{8,9},{9,8},{10,11... | collective-permute-start | bytes 147464 | tf_op jit(solution)/shard_map/ppermute | solution.py:434
  44.6 3.7 %collective-permute-start.14 = (f32[16,128]{1,0:T(8,128)S(1)}, f32[16,128]{1,0:T(8,128)S(1)}, u32[]{:S(2)}, u32[]{:S(2)}) collective-permute-start(f32[16,128]{1,0:T(8,128)S(1)} %shard_map.105.refs_0_), channel_id=1, source_target_pairs={{0,8},{8,0},{16,24},{24,16},{1,9},{9,1},{17,25},{25,17},{2,10},{10... | collective-permute-start | bytes 24584 | tf_op jit(solution)/shard_map/ppermute | solution.py:434
  45.9 3.7 %collective-permute-start.15 = (f32[16,128]{1,0:T(8,128)S(1)}, f32[16,128]{1,0:T(8,128)S(1)}, u32[]{:S(2)}, u32[]{:S(2)}) collective-permute-start(f32[16,128]{1,0:T(8,128)S(1)} %shard_map.105.refs_0_), channel_id=1, source_target_pairs={{0,16},{8,24},{16,0},{24,8},{1,17},{9,25},{17,1},{25,9},{2,18},{10... | collective-permute-start | bytes 24584 | tf_op jit(solution)/shard_map/ppermute | solution.py:434
  48.4 3.7 %collective-permute-start.16 = (f32[16,128]{1,0:T(8,128)S(1)}, f32[16,128]{1,0:T(8,128)S(1)}, u32[]{:S(2)}, u32[]{:S(2)}) collective-permute-start(f32[16,128]{1,0:T(8,128)S(1)} %collective-permute-done.14.refs_1_), channel_id=1, source_target_pairs={{0,16},{8,24},{16,0},{24,8},{1,17},{9,25},{17,1},{25,9},{2,18},{10... | collective-permute-start | bytes 24584 | tf_op jit(solution)/shard_map/ppermute | solution.py:434
  55.5 7.9 %collective-permute-start.18 = (f32[96,128]{1,0:T(8,128)S(1)}, f32[96,128]{1,0:T(8,128)S(1)}, u32[]{:S(2)}, u32[]{:S(2)}) collective-permute-start(f32[96,128]{1,0:T(8,128)S(1)} %get-tuple-element.50), channel_id=1, source_target_pairs={{0,2},{1,3},{2,0},{3,1},{4,6},{5,7},{6,4},{7,5},{8,10},{9,11},{10,... | collective-permute-start | bytes 147464 | tf_op jit(solution)/shard_map/ppermute | solution.py:434
  56.2 7.2 %collective-permute-start.19 = (f32[96,128]{1,0:T(8,128)S(1)}, f32[96,128]{1,0:T(8,128)S(1)}, u32[]{:S(2)}, u32[]{:S(2)}) collective-permute-start(f32[96,128]{1,0:T(8,128)S(1)} %get-tuple-element.51), channel_id=1, source_target_pairs={{0,4},{1,5},{2,6},{3,7},{4,0},{5,1},{6,2},{7,3},{8,12},{9,13},{10,... | collective-permute-start | bytes 147464 | tf_op jit(solution)/shard_map/ppermute | solution.py:434
  57.7 5.9 %collective-permute-start.20 = (f32[96,128]{1,0:T(8,128)S(1)}, f32[96,128]{1,0:T(8,128)S(1)}, u32[]{:S(2)}, u32[]{:S(2)}) collective-permute-start(f32[96,128]{1,0:T(8,128)S(1)} %get-tuple-element.52), channel_id=1, source_target_pairs={{0,6},{1,7},{2,4},{3,5},{4,2},{5,3},{6,0},{7,1},{8,14},{9,15},{10,... | collective-permute-start | bytes 147464 | tf_op jit(solution)/shard_map/ppermute | solution.py:434
  63.6 4.5 %collective-permute-start.21 = (f32[96,128]{1,0:T(8,128)S(1)}, f32[96,128]{1,0:T(8,128)S(1)}, u32[]{:S(2)}, u32[]{:S(2)}) collective-permute-start(f32[96,128]{1,0:T(8,128)S(1)} %shard_map.110.refs_0_.old), channel_id=1, source_target_pairs={{0,2},{1,3},{2,0},{3,1},{4,6},{5,7},{6,4},{7,5},{8,10},{9,11},{10,... | collective-permute-start | bytes 147464 | tf_op jit(solution)/shard_map/ppermute | solution.py:434
  64.3 6.0 %collective-permute-start.23 = (f32[96,128]{1,0:T(8,128)S(1)}, f32[96,128]{1,0:T(8,128)S(1)}, u32[]{:S(2)}, u32[]{:S(2)}) collective-permute-start(f32[96,128]{1,0:T(8,128)S(1)} %shard_map.110.refs_0_.old), channel_id=1, source_target_pairs={{0,4},{1,5},{2,6},{3,7},{4,0},{5,1},{6,2},{7,3},{8,12},{9,13},{10,... | collective-permute-start | bytes 147464 | tf_op jit(solution)/shard_map/ppermute | solution.py:434
  66.5 5.9 %collective-permute-start.25 = (f32[96,128]{1,0:T(8,128)S(1)}, f32[96,128]{1,0:T(8,128)S(1)}, u32[]{:S(2)}, u32[]{:S(2)}) collective-permute-start(f32[96,128]{1,0:T(8,128)S(1)} %shard_map.110.refs_0_.old), channel_id=1, source_target_pairs={{0,6},{1,7},{2,4},{3,5},{4,2},{5,3},{6,0},{7,1},{8,14},{9,15},{10,... | collective-permute-start | bytes 147464 | tf_op jit(solution)/shard_map/ppermute | solution.py:434
  68.0 4.4 %collective-permute-start.27 = (f32[96,128]{1,0:T(8,128)S(1)}, f32[96,128]{1,0:T(8,128)S(1)}, u32[]{:S(2)}, u32[]{:S(2)}) collective-permute-start(f32[96,128]{1,0:T(8,128)S(1)} %shard_map.110.refs_0_.old), channel_id=1, source_target_pairs={{0,1},{1,0},{2,3},{3,2},{4,5},{5,4},{6,7},{7,6},{8,9},{9,8},{10,11... | collective-permute-start | bytes 147464 | tf_op jit(solution)/shard_map/ppermute | solution.py:434
  68.0 7.2 %collective-permute-start.22 = (f32[96,128]{1,0:T(8,128)S(1)}, f32[96,128]{1,0:T(8,128)S(1)}, u32[]{:S(2)}, u32[]{:S(2)}) collective-permute-start(f32[96,128]{1,0:T(8,128)S(1)} %collective-permute-done.21.refs_0_), channel_id=1, source_target_pairs={{0,1},{1,0},{2,3},{3,2},{4,5},{5,4},{6,7},{7,6},{8,9},{9,8},{10,11... | collective-permute-start | bytes 147464 | tf_op jit(solution)/shard_map/ppermute | solution.py:434
  70.3 4.9 %collective-permute-start.24 = (f32[96,128]{1,0:T(8,128)S(1)}, f32[96,128]{1,0:T(8,128)S(1)}, u32[]{:S(2)}, u32[]{:S(2)}) collective-permute-start(f32[96,128]{1,0:T(8,128)S(1)} %collective-permute-done.23.refs_1_), channel_id=1, source_target_pairs={{0,1},{1,0},{2,3},{3,2},{4,5},{5,4},{6,7},{7,6},{8,9},{9,8},{10,11... | collective-permute-start | bytes 147464 | tf_op jit(solution)/shard_map/ppermute | solution.py:434
  72.4 2.8 %collective-permute-start.26 = (f32[96,128]{1,0:T(8,128)S(1)}, f32[96,128]{1,0:T(8,128)S(1)}, u32[]{:S(2)}, u32[]{:S(2)}) collective-permute-start(f32[96,128]{1,0:T(8,128)S(1)} %collective-permute-done.25.refs_2_), channel_id=1, source_target_pairs={{0,1},{1,0},{2,3},{3,2},{4,5},{5,4},{6,7},{7,6},{8,9},{9,8},{10,11... | collective-permute-start | bytes 147464 | tf_op jit(solution)/shard_map/ppermute | solution.py:434
  76.7 3.7 %collective-permute-start.28 = (f32[16,128]{1,0:T(8,128)S(1)}, f32[16,128]{1,0:T(8,128)S(1)}, u32[]{:S(2)}, u32[]{:S(2)}) collective-permute-start(f32[16,128]{1,0:T(8,128)S(1)} %shard_map.114.refs_0_), channel_id=1, source_target_pairs={{0,8},{8,0},{16,24},{24,16},{1,9},{9,1},{17,25},{25,17},{2,10},{10... | collective-permute-start | bytes 24584 | tf_op jit(solution)/shard_map/ppermute | solution.py:434
  77.5 3.7 %collective-permute-start.29 = (f32[16,128]{1,0:T(8,128)S(1)}, f32[16,128]{1,0:T(8,128)S(1)}, u32[]{:S(2)}, u32[]{:S(2)}) collective-permute-start(f32[16,128]{1,0:T(8,128)S(1)} %shard_map.114.refs_0_), channel_id=1, source_target_pairs={{0,16},{8,24},{16,0},{24,8},{1,17},{9,25},{17,1},{25,9},{2,18},{10... | collective-permute-start | bytes 24584 | tf_op jit(solution)/shard_map/ppermute | solution.py:434
  80.4 3.7 %collective-permute-start.30 = (f32[16,128]{1,0:T(8,128)S(1)}, f32[16,128]{1,0:T(8,128)S(1)}, u32[]{:S(2)}, u32[]{:S(2)}) collective-permute-start(f32[16,128]{1,0:T(8,128)S(1)} %collective-permute-done.28.refs_1_), channel_id=1, source_target_pairs={{0,16},{8,24},{16,0},{24,8},{1,17},{9,25},{17,1},{25,9},{2,18},{10... | collective-permute-start | bytes 24584 | tf_op jit(solution)/shard_map/ppermute | solution.py:434
  87.5 5.1 %collective-permute-start.32 = (f32[96,128]{1,0:T(8,128)S(1)}, f32[96,128]{1,0:T(8,128)S(1)}, u32[]{:S(2)}, u32[]{:S(2)}) collective-permute-start(f32[96,128]{1,0:T(8,128)S(1)} %get-tuple-element.59), channel_id=1, source_target_pairs={{0,2},{1,3},{2,0},{3,1},{4,6},{5,7},{6,4},{7,5},{8,10},{9,11},{10,... | collective-permute-start | bytes 147464 | tf_op jit(solution)/shard_map/ppermute | solution.py:434
  87.6 5.7 %collective-permute-start.33 = (f32[96,128]{1,0:T(8,128)S(1)}, f32[96,128]{1,0:T(8,128)S(1)}, u32[]{:S(2)}, u32[]{:S(2)}) collective-permute-start(f32[96,128]{1,0:T(8,128)S(1)} %get-tuple-element.60), channel_id=1, source_target_pairs={{0,4},{1,5},{2,6},{3,7},{4,0},{5,1},{6,2},{7,3},{8,12},{9,13},{10,... | collective-permute-start | bytes 147464 | tf_op jit(solution)/shard_map/ppermute | solution.py:434
  89.7 5.9 %collective-permute-start.34 = (f32[96,128]{1,0:T(8,128)S(1)}, f32[96,128]{1,0:T(8,128)S(1)}, u32[]{:S(2)}, u32[]{:S(2)}) collective-permute-start(f32[96,128]{1,0:T(8,128)S(1)} %get-tuple-element.61), channel_id=1, source_target_pairs={{0,6},{1,7},{2,4},{3,5},{4,2},{5,3},{6,0},{7,1},{8,14},{9,15},{10,... | collective-permute-start | bytes 147464 | tf_op jit(solution)/shard_map/ppermute | solution.py:434
  (5 other events, 37.9 us)
where the time goes:
time: 96.4 us; the launch traced here: 96.2 us
  Pallas kernels  37.2 us (39%)
  starting transfers between devices  31.3 us (32%)
  waiting for transfers between devices  26.8 us (28%)
    pallas_call x25, Pallas kernels, call(): pl.pallas_call(kernel, out_shape=outs, in_specs=specs or [in_vmem] * len(...  37.2 us
    ppermute x35, starting transfers between devices, exchange(): return lax.ppermute(array, axis, [(i, i ^ offset) for i in range(size)])  31.3 us
    ppermute x35, waiting for transfers between devices, exchange(): return lax.ppermute(array, axis, [(i, i ^ offset) for i in range(size)])  26.8 us
  transfers between devices with their start and end apart: 35, of which 17 were waited for; matrix products, arithmetic and copies ran while one was open for 0% of the time, Pallas kernels for 20%

commit v1 on v0

--- a/solution.py
+++ b/solution.py
@@ -256,10 +256,7 @@
 
 
 def group_size(tiles):
-    size = 32
-    while tiles % size:
-        size //= 2
-    return size
+    return next(size for size in (48, 32, 16, BLOCK) if tiles % size == 0)
 
 
 def spread_half(step, odd, rows_ref, limits, change_ref, out):

time: 96.4 us -> 95.1 us (0.987)
  Pallas kernels: 37.2 us -> 36 us
    pallas_call x25, Pallas kernels: 37.2 us -> 36 us  [call(): pl.pallas_call(kernel, out_shape=outs, in_specs=specs or [in_vmem] * len(...]
where the time goes in v1:
time: 95.1 us; the launch traced here: 94.9 us
  Pallas kernels  36 us (38%)
  starting transfers between devices  31 us (33%)
  waiting for transfers between devices  27 us (28%)
    pallas_call x25, Pallas kernels, call(): pl.pallas_call(kernel, out_shape=outs, in_specs=specs or [in_vmem] * len(...  36 us
    ppermute x35, starting transfers between devices, exchange(): return lax.ppermute(array, axis, [(i, i ^ offset) for i in range(size)])  31 us
    ppermute x35, waiting for transfers between devices, exchange(): return lax.ppermute(array, axis, [(i, i ^ offset) for i in range(size)])  27 us
  transfers between devices with their start and end apart: 35, of which 17 were waited for; matrix products, arithmetic and copies ran while one was open for 0% of the time, Pallas kernels for 20%

profile of v1, /device:TPU:0, one launch (start us, length us, event | category | flops | bytes accessed | tf_op | source)
XLA Modules:
  0.0 94.9 jit_solution(10405945828246287381)
XLA Ops:
  0.7 10.2 %shard_map.95 = (bf16[96,98304]{1,0:T(8,128)(2,1)S(1)}, f32[16,128]{1,0:T(8,128)S(1)}, s32[8,128]{1,0:T(8,128)S(1)}, f32[96,128]{1,0:T(8,128)S(1)}, f32[30,128]{1,0:T(8,128)S(1)}, /*index=5*/f32[96,128]{1,0:T(8,128)S(1)}) custom-call(bf16[128,98304]{1,0:T(8,128)(2,1)} %genotypes_hbm.1, f32[768,128]{1,0:T(8,128)} %bitcast.8, s32[768,128]{1,0:T(8,128)} %bitcast.9, ...), custom_call_target="tpu_custom_call" | custom-call | tf_op jit(solution)/shard_map/pallas_call | solution.py:419
  10.8 2.7 %collective-permute-start = (f32[16,128]{1,0:T(8,128)S(1)}, f32[16,128]{1,0:T(8,128)S(1)}, u32[]{:S(2)}, u32[]{:S(2)}) collective-permute-start(f32[16,128]{1,0:T(8,128)S(1)} %get-tuple-element.38.refs_0_), channel_id=1, source_target_pairs={{0,8},{8,0},{16,24},{24,16},{1,9},{9,1},{17,25},{25,17},{2,10},{10... | collective-permute-start | bytes 24584 | tf_op jit(solution)/shard_map/ppermute | solution.py:431
  15.1 1.6 %collective-permute-start.2 = (f32[16,128]{1,0:T(8,128)S(1)}, f32[16,128]{1,0:T(8,128)S(1)}, u32[]{:S(2)}, u32[]{:S(2)}) collective-permute-start(f32[16,128]{1,0:T(8,128)S(1)} %collective-permute-done.refs_1_), channel_id=1, source_target_pairs={{0,16},{8,24},{16,0},{24,8},{1,17},{9,25},{17,1},{25,9},{2,18},{10... | collective-permute-start | bytes 24584 | tf_op jit(solution)/shard_map/ppermute | solution.py:431
  17.1 1.6 %collective-permute-done.2.refs_3_ = f32[16,128]{1,0:T(8,128)S(1)} collective-permute-done((f32[16,128]{1,0:T(8,128)S(1)}, f32[16,128]{1,0:T(8,128)S(1)}, u32[]{:S(2)}, u32[]{:S(2)}) %collective-permute-start.2) | collective-permute-done | bytes 8224 | tf_op jit(solution)/shard_map/ppermute | solution.py:431
  18.8 1.3 %shard_map.97 = (f32[4,96,128]{2,1,0:T(8,128)S(1)}, f32[5,32,128]{2,1,0:T(8,128)S(1)}, f32[5,32,128]{2,1,0:T(8,128)S(1)}) custom-call(bf16[96,98304]{1,0:T(8,128)(2,1)S(1)} %get-tuple-element.34.rows_ref, s32[8,128]{1,0:T(8,128)S(1)} %get-tuple-element.35.limits, f32[10,32,128]{2,1,0:T(8,128)S(1)} %shard_map.96.columns, ...), custom_call_target="tpu_custom_call" | custom-call | tf_op jit(solution)/shard_map/pallas_call | solution.py:419
  20.2 1.8 %shard_map.98.keep = f32[4,96,128]{2,1,0:T(8,128)S(1)} custom-call(bf16[96,98304]{1,0:T(8,128)(2,1)S(1)} %get-tuple-element.34.rows_ref, s32[8,128]{1,0:T(8,128)S(1)} %get-tuple-element.35.limits, f32[5,32,128]{2,1,0:T(8,128)S(1)} %get-tuple-element.39.change_ref), custom_call_target="tpu_custom_call" | custom-call | tf_op jit(solution)/shard_map/pallas_call | solution.py:419
  22.0 2.5 %collective-permute-start.4 = (f32[96,128]{1,0:T(8,128)S(1)}, f32[96,128]{1,0:T(8,128)S(1)}, u32[]{:S(2)}, u32[]{:S(2)}) collective-permute-start(f32[96,128]{1,0:T(8,128)S(1)} %get-tuple-element.42), channel_id=1, source_target_pairs={{0,2},{1,3},{2,0},{3,1},{4,6},{5,7},{6,4},{7,5},{8,10},{9,11},{10,... | collective-permute-start | bytes 147464 | tf_op jit(solution)/shard_map/ppermute | solution.py:431
  24.6 2.6 %collective-permute-start.5 = (f32[96,128]{1,0:T(8,128)S(1)}, f32[96,128]{1,0:T(8,128)S(1)}, u32[]{:S(2)}, u32[]{:S(2)}) collective-permute-start(f32[96,128]{1,0:T(8,128)S(1)} %get-tuple-element.43), channel_id=1, source_target_pairs={{0,4},{1,5},{2,6},{3,7},{4,0},{5,1},{6,2},{7,3},{8,12},{9,13},{10,... | collective-permute-start | bytes 147464 | tf_op jit(solution)/shard_map/ppermute | solution.py:431
  27.1 3.4 %shard_map.100.refs_4_ = f32[8,128]{1,0:T(8,128)S(1)} custom-call(bf16[96,98304]{1,0:T(8,128)(2,1)S(1)} %get-tuple-element.34.rows_ref, s32[8,128]{1,0:T(8,128)S(1)} %get-tuple-element.35.limits), custom_call_target="tpu_custom_call" | custom-call | tf_op jit(solution)/shard_map/pallas_call | solution.py:419
  30.6 2.5 %collective-permute-done.6.refs_3_ = f32[96,128]{1,0:T(8,128)S(1)} collective-permute-done((f32[96,128]{1,0:T(8,128)S(1)}, f32[96,128]{1,0:T(8,128)S(1)}, u32[]{:S(2)}, u32[]{:S(2)}) %collective-permute-start.6) | collective-permute-done | bytes 49184 | tf_op jit(solution)/shard_map/ppermute | solution.py:431
  34.7 1.9 %collective-permute-start.7 = (f32[96,128]{1,0:T(8,128)S(1)}, f32[96,128]{1,0:T(8,128)S(1)}, u32[]{:S(2)}, u32[]{:S(2)}) collective-permute-start(f32[96,128]{1,0:T(8,128)S(1)} %shard_map.101.refs_0_.old), channel_id=1, source_target_pairs={{0,2},{1,3},{2,0},{3,1},{4,6},{5,7},{6,4},{7,5},{8,10},{9,11},{10,... | collective-permute-start | bytes 147464 | tf_op jit(solution)/shard_map/ppermute | solution.py:431
  36.6 1.5 %collective-permute-done.9.refs_1_ = f32[96,128]{1,0:T(8,128)S(1)} collective-permute-done((f32[96,128]{1,0:T(8,128)S(1)}, f32[96,128]{1,0:T(8,128)S(1)}, u32[]{:S(2)}, u32[]{:S(2)}) %collective-permute-start.9) | collective-permute-done | bytes 49184 | tf_op jit(solution)/shard_map/ppermute | solution.py:431
  41.1 1.6 %shard_map.104.refs_3_ = f32[5,32,128]{2,1,0:T(8,128)S(1)} custom-call(bf16[96,98304]{1,0:T(8,128)(2,1)S(1)} %get-tuple-element.34.rows_ref, s32[8,128]{1,0:T(8,128)S(1)} %get-tuple-element.35.limits, f32[96,128]{1,0:T(8,128)S(1)} %collective-permute-done.7.refs_0_, f32[96,128]{1,0:T(8,128)S(1)} %collective-permute-done.9.refs_1_, ...), custom_call_target="tpu_custom_call" | custom-call | tf_op jit(solution)/shard_map/pallas_call | solution.py:419
  44.0 1.4 %collective-permute-start.14 = (f32[16,128]{1,0:T(8,128)S(1)}, f32[16,128]{1,0:T(8,128)S(1)}, u32[]{:S(2)}, u32[]{:S(2)}) collective-permute-start(f32[16,128]{1,0:T(8,128)S(1)} %shard_map.105.refs_0_), channel_id=1, source_target_pairs={{0,8},{8,0},{16,24},{24,16},{1,9},{9,1},{17,25},{25,17},{2,10},{10... | collective-permute-start | bytes 24584 | tf_op jit(solution)/shard_map/ppermute | solution.py:431
  45.4 2.3 %collective-permute-done.14.refs_1_ = f32[16,128]{1,0:T(8,128)S(1)} collective-permute-done((f32[16,128]{1,0:T(8,128)S(1)}, f32[16,128]{1,0:T(8,128)S(1)}, u32[]{:S(2)}, u32[]{:S(2)}) %collective-permute-start.14) | collective-permute-done | bytes 8224 | tf_op jit(solution)/shard_map/ppermute | solution.py:431
  49.0 2.4 %collective-permute-done.16.refs_3_ = f32[16,128]{1,0:T(8,128)S(1)} collective-permute-done((f32[16,128]{1,0:T(8,128)S(1)}, f32[16,128]{1,0:T(8,128)S(1)}, u32[]{:S(2)}, u32[]{:S(2)}) %collective-permute-start.16) | collective-permute-done | bytes 8224 | tf_op jit(solution)/shard_map/ppermute | solution.py:431
  51.4 1.3 %shard_map.106 = (f32[4,96,128]{2,1,0:T(8,128)S(1)}, f32[5,32,128]{2,1,0:T(8,128)S(1)}, f32[5,32,128]{2,1,0:T(8,128)S(1)}) custom-call(bf16[96,98304]{1,0:T(8,128)(2,1)S(1)} %get-tuple-element.34.rows_ref, s32[8,128]{1,0:T(8,128)S(1)} %get-tuple-element.35.limits, f32[10,32,128]{2,1,0:T(8,128)S(1)} %get-tuple-element.46.columns, ...), custom_call_target="tpu_custom_call" | custom-call | tf_op jit(solution)/shard_map/pallas_call | solution.py:419
  52.8 1.8 %shard_map.107.keep = f32[4,96,128]{2,1,0:T(8,128)S(1)} custom-call(bf16[96,98304]{1,0:T(8,128)(2,1)S(1)} %get-tuple-element.34.rows_ref, s32[8,128]{1,0:T(8,128)S(1)} %get-tuple-element.35.limits, f32[5,32,128]{2,1,0:T(8,128)S(1)} %get-tuple-element.47.change_ref), custom_call_target="tpu_custom_call" | custom-call | tf_op jit(solution)/shard_map/pallas_call | solution.py:419
  55.4 1.3 %collective-permute-start.19 = (f32[96,128]{1,0:T(8,128)S(1)}, f32[96,128]{1,0:T(8,128)S(1)}, u32[]{:S(2)}, u32[]{:S(2)}) collective-permute-start(f32[96,128]{1,0:T(8,128)S(1)} %get-tuple-element.51), channel_id=1, source_target_pairs={{0,4},{1,5},{2,6},{3,7},{4,0},{5,1},{6,2},{7,3},{8,12},{9,13},{10,... | collective-permute-start | bytes 147464 | tf_op jit(solution)/shard_map/ppermute | solution.py:431
  56.7 2.3 %collective-permute-start.20 = (f32[96,128]{1,0:T(8,128)S(1)}, f32[96,128]{1,0:T(8,128)S(1)}, u32[]{:S(2)}, u32[]{:S(2)}) collective-permute-start(f32[96,128]{1,0:T(8,128)S(1)} %get-tuple-element.52), channel_id=1, source_target_pairs={{0,6},{1,7},{2,4},{3,5},{4,2},{5,3},{6,0},{7,1},{8,14},{9,15},{10,... | collective-permute-start | bytes 147464 | tf_op jit(solution)/shard_map/ppermute | solution.py:431
  59.1 3.4 %shard_map.109.refs_4_ = f32[8,128]{1,0:T(8,128)S(1)} custom-call(bf16[96,98304]{1,0:T(8,128)(2,1)S(1)} %get-tuple-element.34.rows_ref, s32[8,128]{1,0:T(8,128)S(1)} %get-tuple-element.35.limits), custom_call_target="tpu_custom_call" | custom-call | tf_op jit(solution)/shard_map/pallas_call | solution.py:419
  63.4 2.2 %collective-permute-start.23 = (f32[96,128]{1,0:T(8,128)S(1)}, f32[96,128]{1,0:T(8,128)S(1)}, u32[]{:S(2)}, u32[]{:S(2)}) collective-permute-start(f32[96,128]{1,0:T(8,128)S(1)} %shard_map.110.refs_0_.old), channel_id=1, source_target_pairs={{0,4},{1,5},{2,6},{3,7},{4,0},{5,1},{6,2},{7,3},{8,12},{9,13},{10,... | collective-permute-start | bytes 147464 | tf_op jit(solution)/shard_map/ppermute | solution.py:431
  65.6 1.6 %collective-permute-start.25 = (f32[96,128]{1,0:T(8,128)S(1)}, f32[96,128]{1,0:T(8,128)S(1)}, u32[]{:S(2)}, u32[]{:S(2)}) collective-permute-start(f32[96,128]{1,0:T(8,128)S(1)} %shard_map.110.refs_0_.old), channel_id=1, source_target_pairs={{0,6},{1,7},{2,4},{3,5},{4,2},{5,3},{6,0},{7,1},{8,14},{9,15},{10,... | collective-permute-start | bytes 147464 | tf_op jit(solution)/shard_map/ppermute | solution.py:431
  68.7 2.8 %collective-permute-done.25.refs_2_ = f32[96,128]{1,0:T(8,128)S(1)} collective-permute-done((f32[96,128]{1,0:T(8,128)S(1)}, f32[96,128]{1,0:T(8,128)S(1)}, u32[]{:S(2)}, u32[]{:S(2)}) %collective-permute-start.25) | collective-permute-done | bytes 49184 | tf_op jit(solution)/shard_map/ppermute | solution.py:431
  72.7 1.6 %shard_map.113.refs_3_ = f32[5,32,128]{2,1,0:T(8,128)S(1)} custom-call(bf16[96,98304]{1,0:T(8,128)(2,1)S(1)} %get-tuple-element.34.rows_ref, s32[8,128]{1,0:T(8,128)S(1)} %get-tuple-element.35.limits, f32[96,128]{1,0:T(8,128)S(1)} %collective-permute-done.21.refs_0_, f32[96,128]{1,0:T(8,128)S(1)} %collective-permute-done.23.refs_1_, ...), custom_call_target="tpu_custom_call" | custom-call | tf_op jit(solution)/shard_map/pallas_call | solution.py:419
  76.4 2.8 %collective-permute-done.28.refs_1_ = f32[16,128]{1,0:T(8,128)S(1)} collective-permute-done((f32[16,128]{1,0:T(8,128)S(1)}, f32[16,128]{1,0:T(8,128)S(1)}, u32[]{:S(2)}, u32[]{:S(2)}) %collective-permute-start.28) | collective-permute-done | bytes 8224 | tf_op jit(solution)/shard_map/ppermute | solution.py:431
  80.1 2.8 %collective-permute-done.30.refs_3_ = f32[16,128]{1,0:T(8,128)S(1)} collective-permute-done((f32[16,128]{1,0:T(8,128)S(1)}, f32[16,128]{1,0:T(8,128)S(1)}, u32[]{:S(2)}, u32[]{:S(2)}) %collective-permute-start.30) | collective-permute-done | bytes 8224 | tf_op jit(solution)/shard_map/ppermute | solution.py:431
  82.9 1.3 %shard_map.115 = (f32[4,96,128]{2,1,0:T(8,128)S(1)}, f32[5,32,128]{2,1,0:T(8,128)S(1)}, f32[5,32,128]{2,1,0:T(8,128)S(1)}) custom-call(bf16[96,98304]{1,0:T(8,128)(2,1)S(1)} %get-tuple-element.34.rows_ref, s32[8,128]{1,0:T(8,128)S(1)} %get-tuple-element.35.limits, f32[10,32,128]{2,1,0:T(8,128)S(1)} %get-tuple-element.55.columns, ...), custom_call_target="tpu_custom_call" | custom-call | tf_op jit(solution)/shard_map/pallas_call | solution.py:419
  84.3 1.8 %shard_map.116.keep = f32[4,96,128]{2,1,0:T(8,128)S(1)} custom-call(bf16[96,98304]{1,0:T(8,128)(2,1)S(1)} %get-tuple-element.34.rows_ref, s32[8,128]{1,0:T(8,128)S(1)} %get-tuple-element.35.limits, f32[5,32,128]{2,1,0:T(8,128)S(1)} %get-tuple-element.56.change_ref), custom_call_target="tpu_custom_call" | custom-call | tf_op jit(solution)/shard_map/pallas_call | solution.py:419
  86.2 2.2 %collective-permute-start.33 = (f32[96,128]{1,0:T(8,128)S(1)}, f32[96,128]{1,0:T(8,128)S(1)}, u32[]{:S(2)}, u32[]{:S(2)}) collective-permute-start(f32[96,128]{1,0:T(8,128)S(1)} %get-tuple-element.60), channel_id=1, source_target_pairs={{0,4},{1,5},{2,6},{3,7},{4,0},{5,1},{6,2},{7,3},{8,12},{9,13},{10,... | collective-permute-start | bytes 147464 | tf_op jit(solution)/shard_map/ppermute | solution.py:431
  88.4 2.2 %collective-permute-start.34 = (f32[96,128]{1,0:T(8,128)S(1)}, f32[96,128]{1,0:T(8,128)S(1)}, u32[]{:S(2)}, u32[]{:S(2)}) collective-permute-start(f32[96,128]{1,0:T(8,128)S(1)} %get-tuple-element.61), channel_id=1, source_target_pairs={{0,6},{1,7},{2,4},{3,5},{4,2},{5,3},{6,0},{7,1},{8,14},{9,15},{10,... | collective-permute-start | bytes 147464 | tf_op jit(solution)/shard_map/ppermute | solution.py:431
  91.8 2.5 %collective-permute-done.34.refs_3_ = f32[96,128]{1,0:T(8,128)S(1)} collective-permute-done((f32[96,128]{1,0:T(8,128)S(1)}, f32[96,128]{1,0:T(8,128)S(1)}, u32[]{:S(2)}, u32[]{:S(2)}) %collective-permute-start.34) | collective-permute-done | bytes 49184 | tf_op jit(solution)/shard_map/ppermute | solution.py:431
  (67 shorter events, 18.9 us)
Async XLA Ops:
  10.8 4.3 %collective-permute-start = (f32[16,128]{1,0:T(8,128)S(1)}, f32[16,128]{1,0:T(8,128)S(1)}, u32[]{:S(2)}, u32[]{:S(2)}) collective-permute-start(f32[16,128]{1,0:T(8,128)S(1)} %get-tuple-element.38.refs_0_), channel_id=1, source_target_pairs={{0,8},{8,0},{16,24},{24,16},{1,9},{9,1},{17,25},{25,17},{2,10},{10... | collective-permute-start | bytes 24584 | tf_op jit(solution)/shard_map/ppermute | solution.py:431
  13.5 3.7 %collective-permute-start.1 = (f32[16,128]{1,0:T(8,128)S(1)}, f32[16,128]{1,0:T(8,128)S(1)}, u32[]{:S(2)}, u32[]{:S(2)}) collective-permute-start(f32[16,128]{1,0:T(8,128)S(1)} %get-tuple-element.38.refs_0_), channel_id=1, source_target_pairs={{0,16},{8,24},{16,0},{24,8},{1,17},{9,25},{17,1},{25,9},{2,18},{10... | collective-permute-start | bytes 24584 | tf_op jit(solution)/shard_map/ppermute | solution.py:431
  15.1 3.7 %collective-permute-start.2 = (f32[16,128]{1,0:T(8,128)S(1)}, f32[16,128]{1,0:T(8,128)S(1)}, u32[]{:S(2)}, u32[]{:S(2)}) collective-permute-start(f32[16,128]{1,0:T(8,128)S(1)} %collective-permute-done.refs_1_), channel_id=1, source_target_pairs={{0,16},{8,24},{16,0},{24,8},{1,17},{9,25},{17,1},{25,9},{2,18},{10... | collective-permute-start | bytes 24584 | tf_op jit(solution)/shard_map/ppermute | solution.py:431
  22.0 8.5 %collective-permute-start.4 = (f32[96,128]{1,0:T(8,128)S(1)}, f32[96,128]{1,0:T(8,128)S(1)}, u32[]{:S(2)}, u32[]{:S(2)}) collective-permute-start(f32[96,128]{1,0:T(8,128)S(1)} %get-tuple-element.42), channel_id=1, source_target_pairs={{0,2},{1,3},{2,0},{3,1},{4,6},{5,7},{6,4},{7,5},{8,10},{9,11},{10,... | collective-permute-start | bytes 147464 | tf_op jit(solution)/shard_map/ppermute | solution.py:431
  24.6 6.0 %collective-permute-start.5 = (f32[96,128]{1,0:T(8,128)S(1)}, f32[96,128]{1,0:T(8,128)S(1)}, u32[]{:S(2)}, u32[]{:S(2)}) collective-permute-start(f32[96,128]{1,0:T(8,128)S(1)} %get-tuple-element.43), channel_id=1, source_target_pairs={{0,4},{1,5},{2,6},{3,7},{4,0},{5,1},{6,2},{7,3},{8,12},{9,13},{10,... | collective-permute-start | bytes 147464 | tf_op jit(solution)/shard_map/ppermute | solution.py:431
  27.1 5.9 %collective-permute-start.6 = (f32[96,128]{1,0:T(8,128)S(1)}, f32[96,128]{1,0:T(8,128)S(1)}, u32[]{:S(2)}, u32[]{:S(2)}) collective-permute-start(f32[96,128]{1,0:T(8,128)S(1)} %get-tuple-element.44), channel_id=1, source_target_pairs={{0,6},{1,7},{2,4},{3,5},{4,2},{5,3},{6,0},{7,1},{8,14},{9,15},{10,... | collective-permute-start | bytes 147464 | tf_op jit(solution)/shard_map/ppermute | solution.py:431
  33.1 5.1 %collective-permute-start.9 = (f32[96,128]{1,0:T(8,128)S(1)}, f32[96,128]{1,0:T(8,128)S(1)}, u32[]{:S(2)}, u32[]{:S(2)}) collective-permute-start(f32[96,128]{1,0:T(8,128)S(1)} %shard_map.101.refs_0_.old), channel_id=1, source_target_pairs={{0,4},{1,5},{2,6},{3,7},{4,0},{5,1},{6,2},{7,3},{8,12},{9,13},{10,... | collective-permute-start | bytes 147464 | tf_op jit(solution)/shard_map/ppermute | solution.py:431
  33.5 5.9 %collective-permute-start.11 = (f32[96,128]{1,0:T(8,128)S(1)}, f32[96,128]{1,0:T(8,128)S(1)}, u32[]{:S(2)}, u32[]{:S(2)}) collective-permute-start(f32[96,128]{1,0:T(8,128)S(1)} %shard_map.101.refs_0_.old), channel_id=1, source_target_pairs={{0,6},{1,7},{2,4},{3,5},{4,2},{5,3},{6,0},{7,1},{8,14},{9,15},{10,... | collective-permute-start | bytes 147464 | tf_op jit(solution)/shard_map/ppermute | solution.py:431
  34.7 4.8 %collective-permute-start.7 = (f32[96,128]{1,0:T(8,128)S(1)}, f32[96,128]{1,0:T(8,128)S(1)}, u32[]{:S(2)}, u32[]{:S(2)}) collective-permute-start(f32[96,128]{1,0:T(8,128)S(1)} %shard_map.101.refs_0_.old), channel_id=1, source_target_pairs={{0,2},{1,3},{2,0},{3,1},{4,6},{5,7},{6,4},{7,5},{8,10},{9,11},{10,... | collective-permute-start | bytes 147464 | tf_op jit(solution)/shard_map/ppermute | solution.py:431
  36.6 3.3 %collective-permute-start.13 = (f32[96,128]{1,0:T(8,128)S(1)}, f32[96,128]{1,0:T(8,128)S(1)}, u32[]{:S(2)}, u32[]{:S(2)}) collective-permute-start(f32[96,128]{1,0:T(8,128)S(1)} %shard_map.101.refs_0_.old), channel_id=1, source_target_pairs={{0,1},{1,0},{2,3},{3,2},{4,5},{5,4},{6,7},{7,6},{8,9},{9,8},{10,11... | collective-permute-start | bytes 147464 | tf_op jit(solution)/shard_map/ppermute | solution.py:431
  38.1 4.6 %collective-permute-start.10 = (f32[96,128]{1,0:T(8,128)S(1)}, f32[96,128]{1,0:T(8,128)S(1)}, u32[]{:S(2)}, u32[]{:S(2)}) collective-permute-start(f32[96,128]{1,0:T(8,128)S(1)} %collective-permute-done.9.refs_1_), channel_id=1, source_target_pairs={{0,1},{1,0},{2,3},{3,2},{4,5},{5,4},{6,7},{7,6},{8,9},{9,8},{10,11... | collective-permute-start | bytes 147464 | tf_op jit(solution)/shard_map/ppermute | solution.py:431
  39.4 3.3 %collective-permute-start.12 = (f32[96,128]{1,0:T(8,128)S(1)}, f32[96,128]{1,0:T(8,128)S(1)}, u32[]{:S(2)}, u32[]{:S(2)}) collective-permute-start(f32[96,128]{1,0:T(8,128)S(1)} %collective-permute-done.11.refs_2_), channel_id=1, source_target_pairs={{0,1},{1,0},{2,3},{3,2},{4,5},{5,4},{6,7},{7,6},{8,9},{9,8},{10,11... | collective-permute-start | bytes 147464 | tf_op jit(solution)/shard_map/ppermute | solution.py:431
  39.4 3.3 %collective-permute-start.8 = (f32[96,128]{1,0:T(8,128)S(1)}, f32[96,128]{1,0:T(8,128)S(1)}, u32[]{:S(2)}, u32[]{:S(2)}) collective-permute-start(f32[96,128]{1,0:T(8,128)S(1)} %collective-permute-done.7.refs_0_), channel_id=1, source_target_pairs={{0,1},{1,0},{2,3},{3,2},{4,5},{5,4},{6,7},{7,6},{8,9},{9,8},{10,11... | collective-permute-start | bytes 147464 | tf_op jit(solution)/shard_map/ppermute | solution.py:431
  44.0 3.7 %collective-permute-start.14 = (f32[16,128]{1,0:T(8,128)S(1)}, f32[16,128]{1,0:T(8,128)S(1)}, u32[]{:S(2)}, u32[]{:S(2)}) collective-permute-start(f32[16,128]{1,0:T(8,128)S(1)} %shard_map.105.refs_0_), channel_id=1, source_target_pairs={{0,8},{8,0},{16,24},{24,16},{1,9},{9,1},{17,25},{25,17},{2,10},{10... | collective-permute-start | bytes 24584 | tf_op jit(solution)/shard_map/ppermute | solution.py:431
  45.3 3.7 %collective-permute-start.15 = (f32[16,128]{1,0:T(8,128)S(1)}, f32[16,128]{1,0:T(8,128)S(1)}, u32[]{:S(2)}, u32[]{:S(2)}) collective-permute-start(f32[16,128]{1,0:T(8,128)S(1)} %shard_map.105.refs_0_), channel_id=1, source_target_pairs={{0,16},{8,24},{16,0},{24,8},{1,17},{9,25},{17,1},{25,9},{2,18},{10... | collective-permute-start | bytes 24584 | tf_op jit(solution)/shard_map/ppermute | solution.py:431
  47.7 3.7 %collective-permute-start.16 = (f32[16,128]{1,0:T(8,128)S(1)}, f32[16,128]{1,0:T(8,128)S(1)}, u32[]{:S(2)}, u32[]{:S(2)}) collective-permute-start(f32[16,128]{1,0:T(8,128)S(1)} %collective-permute-done.14.refs_1_), channel_id=1, source_target_pairs={{0,16},{8,24},{16,0},{24,8},{1,17},{9,25},{17,1},{25,9},{2,18},{10... | collective-permute-start | bytes 24584 | tf_op jit(solution)/shard_map/ppermute | solution.py:431
  54.6 7.8 %collective-permute-start.18 = (f32[96,128]{1,0:T(8,128)S(1)}, f32[96,128]{1,0:T(8,128)S(1)}, u32[]{:S(2)}, u32[]{:S(2)}) collective-permute-start(f32[96,128]{1,0:T(8,128)S(1)} %get-tuple-element.50), channel_id=1, source_target_pairs={{0,2},{1,3},{2,0},{3,1},{4,6},{5,7},{6,4},{7,5},{8,10},{9,11},{10,... | collective-permute-start | bytes 147464 | tf_op jit(solution)/shard_map/ppermute | solution.py:431
  55.4 7.0 %collective-permute-start.19 = (f32[96,128]{1,0:T(8,128)S(1)}, f32[96,128]{1,0:T(8,128)S(1)}, u32[]{:S(2)}, u32[]{:S(2)}) collective-permute-start(f32[96,128]{1,0:T(8,128)S(1)} %get-tuple-element.51), channel_id=1, source_target_pairs={{0,4},{1,5},{2,6},{3,7},{4,0},{5,1},{6,2},{7,3},{8,12},{9,13},{10,... | collective-permute-start | bytes 147464 | tf_op jit(solution)/shard_map/ppermute | solution.py:431
  56.7 6.0 %collective-permute-start.20 = (f32[96,128]{1,0:T(8,128)S(1)}, f32[96,128]{1,0:T(8,128)S(1)}, u32[]{:S(2)}, u32[]{:S(2)}) collective-permute-start(f32[96,128]{1,0:T(8,128)S(1)} %get-tuple-element.52), channel_id=1, source_target_pairs={{0,6},{1,7},{2,4},{3,5},{4,2},{5,3},{6,0},{7,1},{8,14},{9,15},{10,... | collective-permute-start | bytes 147464 | tf_op jit(solution)/shard_map/ppermute | solution.py:431
  62.8 4.5 %collective-permute-start.21 = (f32[96,128]{1,0:T(8,128)S(1)}, f32[96,128]{1,0:T(8,128)S(1)}, u32[]{:S(2)}, u32[]{:S(2)}) collective-permute-start(f32[96,128]{1,0:T(8,128)S(1)} %shard_map.110.refs_0_.old), channel_id=1, source_target_pairs={{0,2},{1,3},{2,0},{3,1},{4,6},{5,7},{6,4},{7,5},{8,10},{9,11},{10,... | collective-permute-start | bytes 147464 | tf_op jit(solution)/shard_map/ppermute | solution.py:431
  63.4 5.3 %collective-permute-start.23 = (f32[96,128]{1,0:T(8,128)S(1)}, f32[96,128]{1,0:T(8,128)S(1)}, u32[]{:S(2)}, u32[]{:S(2)}) collective-permute-start(f32[96,128]{1,0:T(8,128)S(1)} %shard_map.110.refs_0_.old), channel_id=1, source_target_pairs={{0,4},{1,5},{2,6},{3,7},{4,0},{5,1},{6,2},{7,3},{8,12},{9,13},{10,... | collective-permute-start | bytes 147464 | tf_op jit(solution)/shard_map/ppermute | solution.py:431
  65.6 5.9 %collective-permute-start.25 = (f32[96,128]{1,0:T(8,128)S(1)}, f32[96,128]{1,0:T(8,128)S(1)}, u32[]{:S(2)}, u32[]{:S(2)}) collective-permute-start(f32[96,128]{1,0:T(8,128)S(1)} %shard_map.110.refs_0_.old), channel_id=1, source_target_pairs={{0,6},{1,7},{2,4},{3,5},{4,2},{5,3},{6,0},{7,1},{8,14},{9,15},{10,... | collective-permute-start | bytes 147464 | tf_op jit(solution)/shard_map/ppermute | solution.py:431
  67.2 4.3 %collective-permute-start.27 = (f32[96,128]{1,0:T(8,128)S(1)}, f32[96,128]{1,0:T(8,128)S(1)}, u32[]{:S(2)}, u32[]{:S(2)}) collective-permute-start(f32[96,128]{1,0:T(8,128)S(1)} %shard_map.110.refs_0_.old), channel_id=1, source_target_pairs={{0,1},{1,0},{2,3},{3,2},{4,5},{5,4},{6,7},{7,6},{8,9},{9,8},{10,11... | collective-permute-start | bytes 147464 | tf_op jit(solution)/shard_map/ppermute | solution.py:431
  67.2 7.0 %collective-permute-start.22 = (f32[96,128]{1,0:T(8,128)S(1)}, f32[96,128]{1,0:T(8,128)S(1)}, u32[]{:S(2)}, u32[]{:S(2)}) collective-permute-start(f32[96,128]{1,0:T(8,128)S(1)} %collective-permute-done.21.refs_0_), channel_id=1, source_target_pairs={{0,1},{1,0},{2,3},{3,2},{4,5},{5,4},{6,7},{7,6},{8,9},{9,8},{10,11... | collective-permute-start | bytes 147464 | tf_op jit(solution)/shard_map/ppermute | solution.py:431
  68.7 5.6 %collective-permute-start.24 = (f32[96,128]{1,0:T(8,128)S(1)}, f32[96,128]{1,0:T(8,128)S(1)}, u32[]{:S(2)}, u32[]{:S(2)}) collective-permute-start(f32[96,128]{1,0:T(8,128)S(1)} %collective-permute-done.23.refs_1_), channel_id=1, source_target_pairs={{0,1},{1,0},{2,3},{3,2},{4,5},{5,4},{6,7},{7,6},{8,9},{9,8},{10,11... | collective-permute-start | bytes 147464 | tf_op jit(solution)/shard_map/ppermute | solution.py:431
  71.5 2.8 %collective-permute-start.26 = (f32[96,128]{1,0:T(8,128)S(1)}, f32[96,128]{1,0:T(8,128)S(1)}, u32[]{:S(2)}, u32[]{:S(2)}) collective-permute-start(f32[96,128]{1,0:T(8,128)S(1)} %collective-permute-done.25.refs_2_), channel_id=1, source_target_pairs={{0,1},{1,0},{2,3},{3,2},{4,5},{5,4},{6,7},{7,6},{8,9},{9,8},{10,11... | collective-permute-start | bytes 147464 | tf_op jit(solution)/shard_map/ppermute | solution.py:431
  75.5 3.7 %collective-permute-start.28 = (f32[16,128]{1,0:T(8,128)S(1)}, f32[16,128]{1,0:T(8,128)S(1)}, u32[]{:S(2)}, u32[]{:S(2)}) collective-permute-start(f32[16,128]{1,0:T(8,128)S(1)} %shard_map.114.refs_0_), channel_id=1, source_target_pairs={{0,8},{8,0},{16,24},{24,16},{1,9},{9,1},{17,25},{25,17},{2,10},{10... | collective-permute-start | bytes 24584 | tf_op jit(solution)/shard_map/ppermute | solution.py:431
  76.4 3.7 %collective-permute-start.29 = (f32[16,128]{1,0:T(8,128)S(1)}, f32[16,128]{1,0:T(8,128)S(1)}, u32[]{:S(2)}, u32[]{:S(2)}) collective-permute-start(f32[16,128]{1,0:T(8,128)S(1)} %shard_map.114.refs_0_), channel_id=1, source_target_pairs={{0,16},{8,24},{16,0},{24,8},{1,17},{9,25},{17,1},{25,9},{2,18},{10... | collective-permute-start | bytes 24584 | tf_op jit(solution)/shard_map/ppermute | solution.py:431
  79.2 3.7 %collective-permute-start.30 = (f32[16,128]{1,0:T(8,128)S(1)}, f32[16,128]{1,0:T(8,128)S(1)}, u32[]{:S(2)}, u32[]{:S(2)}) collective-permute-start(f32[16,128]{1,0:T(8,128)S(1)} %collective-permute-done.28.refs_1_), channel_id=1, source_target_pairs={{0,16},{8,24},{16,0},{24,8},{1,17},{9,25},{17,1},{25,9},{2,18},{10... | collective-permute-start | bytes 24584 | tf_op jit(solution)/shard_map/ppermute | solution.py:431
  86.1 5.1 %collective-permute-start.32 = (f32[96,128]{1,0:T(8,128)S(1)}, f32[96,128]{1,0:T(8,128)S(1)}, u32[]{:S(2)}, u32[]{:S(2)}) collective-permute-start(f32[96,128]{1,0:T(8,128)S(1)} %get-tuple-element.59), channel_id=1, source_target_pairs={{0,2},{1,3},{2,0},{3,1},{4,6},{5,7},{6,4},{7,5},{8,10},{9,11},{10,... | collective-permute-start | bytes 147464 | tf_op jit(solution)/shard_map/ppermute | solution.py:431
  86.2 5.6 %collective-permute-start.33 = (f32[96,128]{1,0:T(8,128)S(1)}, f32[96,128]{1,0:T(8,128)S(1)}, u32[]{:S(2)}, u32[]{:S(2)}) collective-permute-start(f32[96,128]{1,0:T(8,128)S(1)} %get-tuple-element.60), channel_id=1, source_target_pairs={{0,4},{1,5},{2,6},{3,7},{4,0},{5,1},{6,2},{7,3},{8,12},{9,13},{10,... | collective-permute-start | bytes 147464 | tf_op jit(solution)/shard_map/ppermute | solution.py:431
  88.4 5.9 %collective-permute-start.34 = (f32[96,128]{1,0:T(8,128)S(1)}, f32[96,128]{1,0:T(8,128)S(1)}, u32[]{:S(2)}, u32[]{:S(2)}) collective-permute-start(f32[96,128]{1,0:T(8,128)S(1)} %get-tuple-element.61), channel_id=1, source_target_pairs={{0,6},{1,7},{2,4},{3,5},{4,2},{5,3},{6,0},{7,1},{8,14},{9,15},{10,... | collective-permute-start | bytes 147464 | tf_op jit(solution)/shard_map/ppermute | solution.py:431
  (5 other events, 37.8 us)
